TPU v7x, 512 devices: a whole 4x4x16 slice. The times are simulated.
512 devices in a mesh: grp: 16 (over z_lo, core), row: 32 (over x, y, z_hi).
Axes of the slice: x: 4, y: 4, z: 16 (z_hi: 2, z_lo: 8; z = z_hi * 8 + z_lo), core: 2. Of those that a mesh axis runs over, the one named last changes fastest.
Arguments:
- signal: bfloat16 [2048, 64, 128], P(('grp', 'row')), may hold values from -6 to 6
- leaf_basis: bfloat16 [2048, 64, 128], P(('grp', 'row')), may hold values from -0.5 to 0.5
- near_blocks: bfloat16 [2048, 3, 128, 128], P(('grp', 'row')), may hold values from -0.3125 to 0.3125
- coupling: bfloat16 [98304, 4096], P(('grp', 'row')), may hold values from -0.109375 to 0.109375
- block_cols: int32 [98304], P(('grp', 'row')), may hold values from 0 to 2047, as said below
- block_rows: int32 [98304], P(('grp', 'row')), may hold values from 0 to 3
- block_live: int32 [98304], P(('grp', 'row')), may hold values 0 or 1
Outputs:
- product: bfloat16 [2048, 64, 128], P(('grp', 'row'))
Inputs may be any that keep to these rules, and one draw needn't show every extreme that they name: `block_cols`: slot b of device d (d = b // 192, in group h = d // 32) names a column cluster of group (h + o) mod (16), where o = (b mod 192) // 64 - 1; a group's clusters are g * 128 to (g + 1) * 128 - 1.
All inputs are finite; a program needn't handle non-finite values. No bound on the sum of `block_live` on one device may be relied on, other than what follows from the above.
Results may differ from a plain program's by a relative error of at most 0.0039.
Values may be sent and summed in bfloat16 or wider, within the bound.
A program may use at most 64 MiB of HBM per device.

v0:
```python
import jax
import jax.numpy as jnp
from jax import lax
from jax.sharding import PartitionSpec as P

K = 64
R = 64


def with_halo(block, sides, width, periodic):
    for axis, dim in sides:
        count = lax.axis_size(axis)
        forward = [(i, i + 1) for i in range(count - 1)]
        if periodic:
            forward.append((count - 1, 0))
        backward = [(target, source) for source, target in forward]
        low = lax.ppermute(
            lax.slice_in_dim(block, block.shape[dim] - width, None, axis=dim), axis, forward
        )
        high = lax.ppermute(lax.slice_in_dim(block, 0, width, axis=dim), axis, backward)
        block = jnp.concatenate([low, block, high], axis=dim)
    return block


def per_device(signal, leaf_basis, near_blocks, coupling, block_cols, block_rows, block_live):
    cl_dev = signal.shape[0]
    skeleton = jnp.einsum(
        "crl,ckl->crk", signal, leaf_basis, preferred_element_type=jnp.float32
    ).astype(jnp.bfloat16)
    flat_skel = skeleton.reshape(cl_dev, R * K)
    n_row = lax.axis_size("row")
    n_grp = lax.axis_size("grp")
    group_size = cl_dev * n_row
    panel = lax.all_gather(flat_skel, "row", axis=0, tiled=True)
    window_panel = with_halo(panel, (("grp", 0),), group_size, True)
    my_group = lax.axis_index("grp")
    column_group = block_cols // group_size
    position = (column_group - my_group + 1 + n_grp) % n_grp
    local_ids = position * group_size + block_cols % group_size
    sources = window_panel[local_ids].reshape(-1, R, K)
    sources = sources * block_live.astype(jnp.bfloat16)[:, None, None]
    blocks = coupling.reshape(-1, K, K)
    far_rows = []
    for cluster in range(cl_dev):
        chosen = (block_rows == cluster).astype(jnp.bfloat16)
        masked = sources * chosen[:, None, None]
        far_rows.append(
            jnp.einsum("brm,bkm->rk", masked, blocks, preferred_element_type=jnp.float32)
        )
    far = jnp.stack(far_rows, axis=0)
    far_skeleton = far.astype(jnp.bfloat16)
    total = jnp.einsum("crk,ckl->crl", far_skeleton, leaf_basis, preferred_element_type=jnp.float32)
    padded = with_halo(signal, ((("grp", "row"), 0),), 1, False)
    for index in range(3):
        neighbour = padded[index : index + cl_dev]
        total = total + jnp.einsum(
            "crl,cml->crm", neighbour, near_blocks[:, index], preferred_element_type=jnp.float32
        )
    return total.astype(jnp.bfloat16)


def solution(mesh):
    in_specs = (
        P(("grp", "row"), None, None),
        P(("grp", "row"), None, None),
        P(("grp", "row"), None, None, None),
        P(("grp", "row"), None),
        P(("grp", "row")),
        P(("grp", "row")),
        P(("grp", "row")),
    )
    out_specs = P(("grp", "row"), None, None)
    return jax.shard_map(
        per_device, mesh=mesh, in_specs=in_specs, out_specs=out_specs, check_vma=False
    )
```

profile of v0, /device:TPU:2, one launch (start us, length us, event | category | flops | bytes accessed | tf_op | source)
XLA Modules:
  0.0 215.5 jit_solution(11796397899471478045)
XLA Ops:
  6.6 0.8 copy-done
  7.4 1.0 convolution_convert_fusion
  8.4 0.7 reshape.171
  9.1 117.6 %all-gather.3.cloned.1.call-done = bf16[32,4,4096]{2,1,0:T(4,128)(2,1)} async-done(((bf16[1,4,4096]{2,1,0:T(4,128)(2,1)}), bf16[32,4,4096]{2,1,0:T(4,128)(2,1)}) %all-gather.3.cloned.1.call-update) | async-done | bytes 1048592 | tf_op jit(solution)/shard_map/all_gather | solution.py:34
  126.7 1.3 reshape.172
  128.1 2.1 collective-permute-start
  130.2 10.2 %collective-permute-start.1 = (bf16[128,4096]{1,0:T(8,128)(2,1)S(1)}, bf16[128,4096]{1,0:T(8,128)(2,1)}, u32[]{:S(2)}, u32[]{:S(2)}) collective-permute-start(bf16[128,4096]{1,0:T(8,128)(2,1)S(1)} %reshape.172), channel_id=1, source_target_pairs={{32,0},{64,32},{96,64},{128,96},{160,128},{192,160},{224,192},{256... | collective-permute-start | bytes 3145736 | tf_op jit(solution)/shard_map/ppermute | solution.py:20
  140.4 1.9 collective-permute-start.2
  142.4 15.6 %collective-permute-start.3 = (bf16[1,64,128]{2,1,0:T(8,128)(2,1)S(1)}, bf16[1,64,128]{2,1,0:T(8,128)(2,1)S(1)}, u32[]{:S(2)}, u32[]{:S(2)}) collective-permute-start(bf16[1,64,128]{2,1,0:T(8,128)(2,1)S(1)} %get-tuple-element.9), channel_id=1, source_target_pairs={{1,0},{2,1},{3,2},{4,3},{5,4},{6,5},{7,6},{8,7},{9,8},{10,9},{11,1... | collective-permute-start | bytes 49160 | tf_op jit(solution)/shard_map/ppermute | solution.py:20
  158.1 2.5 %copy.36 = bf16[192,4096]{0,1:T(8,128)(2,1)} copy(bf16[192,4096]{1,0:T(8,128)(2,1)S(1)} %copy-done.4) | data formatting | bytes 3145728 | tf_op args[3]
  160.6 1.1 fusion.75
  161.8 2.0 pad_maximum_fusion
  163.8 2.7 %gather_fusion = bf16[192,4096]{1,0:T(8,128)(2,1)} fusion(bf16[384,4096]{1,0:T(8,128)(2,1)S(1)} %pad_maximum_fusion, s32[1024]{0:T(1024)S(1)} %pad_clamp_fusion), kind=kCustom, calls=%fused_computation | custom fusion | bytes 3146496 | tf_op jit(solution)/shard_map/gather | solution.py:40
  166.5 3.6 %multiply_multiply_fusion.3 = (bf16[192,4096]{1,0:T(8,128)(2,1)}, bf16[192,4096]{1,0:T(8,128)(2,1)}, bf16[192,4096]{1,0:T(8,128)(2,1)S(1)}, bf16[192,4096]{1,0:T(8,128)(2,1)S(1)}) fusion(bf16[192,4096]{1,0:T(8,128)(2,1)} %gather_fusion, bf16[192]{0:T(256)(128)(2,1)S(1)} %get-tuple-element.11, bf16[192]{0:T(256)(128)(2,1)S(1)} %convert_element_type.23, ...), kind=kLoop, calls=%fused_computation.34 | loop fusion | flops 3932160 | bytes 7866240 | tf_op jit(solution)/shard_map/mul | solution.py:46
  170.0 3.8 %copy.35 = bf16[192,4096]{0,1:T(8,128)(2,1)} copy(bf16[192,4096]{1,0:T(8,128)(2,1)} %get-tuple-element.5) | data formatting | bytes 3145728 | tf_op jit(solution)/shard_map/mul | solution.py:46
  173.9 3.8 %copy.39 = bf16[192,4096]{0,1:T(8,128)(2,1)} copy(bf16[192,4096]{1,0:T(8,128)(2,1)} %get-tuple-element.6) | data formatting | bytes 3145728 | tf_op jit(solution)/shard_map/mul | solution.py:46
  177.7 6.8 %fusion.54 = bf16[1,64,64]{2,1,0:T(8,128)(2,1)S(1)} fusion(bf16[192,64,64]{0,2,1:T(8,128)(2,1)} %bitcast.56, bf16[192,64,64]{0,2,1:T(8,128)(2,1)} %bitcast.60), kind=kOutput, calls=%fused_computation.27 | convolution fusion | flops 100667392 | bytes 3153920 | tf_op jit(solution)/shard_map/brm,bkm->rk/dot_general | solution.py:48
  184.6 4.4 %fusion.59 = bf16[1,64,64]{2,1,0:T(8,128)(2,1)S(1)} fusion(bf16[192,64,64]{0,2,1:T(8,128)(2,1)S(1)} %bitcast.59, bf16[192,64,64]{0,2,1:T(8,128)(2,1)S(1)} %bitcast.61), kind=kOutput, calls=%fused_computation.28 | convolution fusion | flops 100667392 | bytes 3153920 | tf_op jit(solution)/shard_map/brm,bkm->rk/dot_general | solution.py:48
  189.0 2.6 %copy.42 = bf16[192,4096]{0,1:T(8,128)(2,1)} copy(bf16[192,4096]{1,0:T(8,128)(2,1)S(1)} %get-tuple-element.7) | data formatting | bytes 3145728 | tf_op jit(solution)/shard_map/mul | solution.py:46
  191.6 6.6 %fusion.64 = bf16[1,64,64]{2,1,0:T(8,128)(2,1)S(1)} fusion(bf16[192,64,64]{0,2,1:T(8,128)(2,1)} %bitcast.57, bf16[192,64,64]{0,2,1:T(8,128)(2,1)} %bitcast.63), kind=kOutput, calls=%fused_computation.29 | convolution fusion | flops 100667392 | bytes 3153920 | tf_op jit(solution)/shard_map/brm,bkm->rk/dot_general | solution.py:48
  198.3 2.5 %copy.45 = bf16[192,4096]{0,1:T(8,128)(2,1)} copy(bf16[192,4096]{1,0:T(8,128)(2,1)S(1)} %get-tuple-element.8) | data formatting | bytes 3145728 | tf_op jit(solution)/shard_map/mul | solution.py:46
  200.7 6.7 %fusion.69 = bf16[1,64,64]{2,1,0:T(8,128)(2,1)S(1)} fusion(bf16[192,64,64]{0,2,1:T(8,128)(2,1)} %bitcast.58, bf16[192,64,64]{0,2,1:T(8,128)(2,1)} %bitcast.62), kind=kOutput, calls=%fused_computation.30 | convolution fusion | flops 100667392 | bytes 3153920 | tf_op jit(solution)/shard_map/brm,bkm->rk/dot_general | solution.py:48
  207.6 0.2 fusion.12
  207.8 0.8 fusion.13
  (31 shorter events, 0.3 us)
Async XLA Ops:
  6.5 0.8 copy-start
  6.5 133.9 %copy-start.5 = (bf16[4,64,128]{2,1,0:T(8,128)(2,1)S(1)}, bf16[4,64,128]{2,1,0:T(8,128)(2,1)}, u32[]{:S(2)}) copy-start(bf16[4,64,128]{2,1,0:T(8,128)(2,1)} %param.7) | copy-start | bytes 196612
  6.5 151.5 %copy-start.9 = (s32[192]{0:T(256)S(1)}, s32[192]{0:T(256)}, u32[]{:S(2)}) copy-start(s32[192]{0:T(256)} %param.13) | copy-start | bytes 2308
  6.5 151.5 %copy-start.4 = (bf16[192,4096]{1,0:T(8,128)(2,1)S(1)}, bf16[192,4096]{1,0:T(8,128)(2,1)}, u32[]{:S(2)}) copy-start(bf16[192,4096]{1,0:T(8,128)(2,1)} %param.10) | copy-start | bytes 4718596
  6.5 120.2 %all-gather.3.cloned.1.call-start = ((), (), s32[]{:S(2)}) async-start(), calls=%async_computation | async-start | bytes 1081344 | tf_op jit(solution)/shard_map/all_gather | solution.py:34
  128.1 33.7 %copy-start.1 = (bf16[128,4096]{1,0:T(8,128)(2,1)}, bf16[128,4096]{1,0:T(8,128)(2,1)S(1)}, u32[]{:S(2)}) copy-start(bf16[128,4096]{1,0:T(8,128)(2,1)S(1)} %reshape.172) | copy-start | bytes 3145732
  128.1 32.5 %copy-start.8 = (s32[192]{0:T(256)S(1)}, s32[192]{0:T(256)}, u32[]{:S(2)}) copy-start(s32[192]{0:T(256)} %param.11) | copy-start | bytes 2308
  128.1 32.5 %copy-start.7 = (s32[192]{0:T(256)S(1)}, s32[192]{0:T(256)}, u32[]{:S(2)}) copy-start(s32[192]{0:T(256)} %param.12) | copy-start | bytes 2308
  128.1 33.6 %collective-permute-start = (bf16[128,4096]{1,0:T(8,128)(2,1)S(1)}, bf16[128,4096]{1,0:T(8,128)(2,1)}, u32[]{:S(2)}, u32[]{:S(2)}) collective-permute-start(bf16[128,4096]{1,0:T(8,128)(2,1)S(1)} %reshape.172), channel_id=1, source_target_pairs={{0,32},{32,64},{64,96},{96,128},{128,160},{160,192},{192,224},{224... | collective-permute-start | bytes 3145736 | tf_op jit(solution)/shard_map/ppermute | solution.py:17
  130.2 31.6 %collective-permute-start.1 = (bf16[128,4096]{1,0:T(8,128)(2,1)S(1)}, bf16[128,4096]{1,0:T(8,128)(2,1)}, u32[]{:S(2)}, u32[]{:S(2)}) collective-permute-start(bf16[128,4096]{1,0:T(8,128)(2,1)S(1)} %reshape.172), channel_id=1, source_target_pairs={{32,0},{64,32},{96,64},{128,96},{160,128},{192,160},{224,192},{256... | collective-permute-start | bytes 3145736 | tf_op jit(solution)/shard_map/ppermute | solution.py:20
  140.4 67.1 %collective-permute-start.2 = (bf16[1,64,128]{2,1,0:T(8,128)(2,1)S(1)}, bf16[1,64,128]{2,1,0:T(8,128)(2,1)S(1)}, u32[]{:S(2)}, u32[]{:S(2)}) collective-permute-start(bf16[1,64,128]{2,1,0:T(8,128)(2,1)S(1)} %get-tuple-element.10), channel_id=1, source_target_pairs={{0,1},{1,2},{2,3},{3,4},{4,5},{5,6},{6,7},{7,8},{8,9},{9,10},{10,1... | collective-permute-start | bytes 49160 | tf_op jit(solution)/shard_map/ppermute | solution.py:17
  142.4 65.4 %collective-permute-start.3 = (bf16[1,64,128]{2,1,0:T(8,128)(2,1)S(1)}, bf16[1,64,128]{2,1,0:T(8,128)(2,1)S(1)}, u32[]{:S(2)}, u32[]{:S(2)}) collective-permute-start(bf16[1,64,128]{2,1,0:T(8,128)(2,1)S(1)} %get-tuple-element.9), channel_id=1, source_target_pairs={{1,0},{2,1},{3,2},{4,3},{5,4},{6,5},{7,6},{8,7},{9,8},{10,9},{11,1... | collective-permute-start | bytes 49160 | tf_op jit(solution)/shard_map/ppermute | solution.py:20
  177.7 6.8 %copy-start.2 = (bf16[192,4096]{0,1:T(8,128)(2,1)S(1)}, bf16[192,4096]{0,1:T(8,128)(2,1)}, u32[]{:S(2)}) copy-start(bf16[192,4096]{0,1:T(8,128)(2,1)} %copy.36) | copy-start | bytes 4718596
  177.7 6.8 %copy-start.3 = (bf16[192,4096]{0,1:T(8,128)(2,1)S(1)}, bf16[192,4096]{0,1:T(8,128)(2,1)}, u32[]{:S(2)}) copy-start(bf16[192,4096]{0,1:T(8,128)(2,1)} %copy.39) | copy-start | bytes 4718596
  200.7 6.9 %copy-start.6 = (bf16[4,3,128,128]{3,2,1,0:T(8,128)(2,1)S(1)}, bf16[4,3,128,128]{3,2,1,0:T(8,128)(2,1)}, u32[]{:S(2)}) copy-start(bf16[4,3,128,128]{3,2,1,0:T(8,128)(2,1)} %param.9) | copy-start | bytes 1179652
Sparse Core Ops, SparseCore 0:
  11.7 115.0 all-gather.2
where the time goes:
time: 216 us; the launch traced here: 215 us
  waiting for transfers between devices  118 us (55%)
  starting transfers between devices  29.9 us (14%)
  matrix products  27.8 us (13%)
  local copies, waits for them, and re-layouts  20.9 us (10%)
  between operations  13.7 us (6%)
  other arithmetic  5.57 us (3%)
    all_gather x1, waiting for transfers between devices, per_device(): panel = lax.all_gather(flat_skel, 'row', axis=0, tiled=True)  118 us
    ppermute x2, starting transfers between devices, with_halo(): lax.ppermute(lax.slice_in_dim(block, 0, width, axis=dim), axis, backward)  25.9 us
    dot_general x4, matrix products, per_device(): jnp.einsum('brm,bkm->rk', masked, blocks, preferred_element_type=jnp.floa...  24.6 us
    mul x4, local copies, waits for them, and re-layouts, per_device(): masked = sources * chosen[:, None, None]  12.8 us
    unnamed x23, local copies, waits for them, and re-layouts  5.42 us
  transfers between devices with their start and end apart: 5, of which 1 were waited for; matrix products, arithmetic and copies ran while one was open for 23% of the time, Pallas kernels for 0%

commit v1 on v0

v1 whole, which is shorter than its diff:
```python
import functools

import jax
import jax.numpy as jnp
from jax import lax
from jax.experimental import pallas as pl
from jax.experimental.pallas import tpu as pltpu
from jax.sharding import PartitionSpec as P

MESH = pl.DeviceIdType.MESH
F32 = jnp.float32
BF16 = jnp.bfloat16

CL = 4
R = 64
LEAF = 128
GSLOTS = 64
HALF = 32
LANES = 128
SIDE = 4


def one_hot(rows, columns, chosen):
    row = lax.broadcasted_iota(jnp.int32, (rows, columns), 0)
    column = lax.broadcasted_iota(jnp.int32, (rows, columns), 1)
    return jnp.where(column == chosen(row), 1.0, 0.0).astype(BF16)


def nt(a, b):
    return lax.dot_general(a, b, (((1,), (1,)), ((), ())), preferred_element_type=F32)


def nn(a, b):
    return jnp.dot(a, b, preferred_element_type=F32)


def kernel(
    nx, ny, nz,
    cols_ref, rows_ref, live_ref, sig_hbm, leaf_hbm, near_hbm, coup_hbm, out_ref,
    sig, leaf, near, coup, own, sibling, neighbour, halo,
    lhs, gathered, acc, total, perm1, perm2, leaf_perm,
    local_sem, send_sem, recv_sem,
):
    grp = lax.axis_index("grp")
    row = lax.axis_index("row")
    n_grp, n_row = 2 * nz, 2 * nx * ny
    z, core = grp // 2, grp % 2
    xy, plane = row // 2, row % 2
    x, y = xy // ny, xy % ny

    def device(x_, y_, plane_):
        return (grp, (x_ * ny + y_) * 2 + plane_)

    opposite = device(x, y, 1 - plane)
    sib = (z * 2 + 1 - core, row)
    step = 2 * core - 1
    z_full = (plane * nz + z + step + 2 * nz) % (2 * nz)
    next_plane = z_full // nz
    near_z = ((z_full % nz) * 2 + 1 - core, xy * 2 + next_plane)
    x_peers = [((x + d) % nx, device((x + d) % nx, y, plane)) for d in range(1, nx)]
    y_peers = [((y + d) % ny, device(x, (y + d) % ny, plane)) for d in range(1, ny)]
    linear = grp * n_row + row
    count = n_grp * n_row
    after, before = (linear + 1) % count, (linear + count - 1) % count
    after_dev = (after // n_row, after % n_row)
    before_dev = (before // n_row, before % n_row)

    mine = pl.ds(plane * CL, CL)
    other_start = (1 - plane) * CL
    next_mine = pl.ds(next_plane * CL, CL)

    stage = []
    for i, (src, dst) in enumerate(((leaf_hbm, leaf), (sig_hbm, sig), (coup_hbm, coup), (near_hbm, near))):
        stage.append(pltpu.make_async_copy(src, dst, local_sem.at[i]))
        stage[-1].start()

    barrier = pltpu.get_barrier_semaphore()
    friends = [opposite, sib, near_z, after_dev, before_dev]
    friends += [dev for _, dev in x_peers] + [dev for _, dev in y_peers]
    for friend in friends:
        pl.semaphore_signal(barrier, inc=1, device_id=friend, device_id_type=MESH)

    stage[0].wait()
    stage[1].wait()
    zero = jnp.zeros((R, LEAF), BF16)
    for c in range(CL):
        a = jnp.concatenate([leaf[c, 0:HALF], leaf[c, HALF : 2 * HALF]], axis=1)
        s = sig[c]
        b = jnp.concatenate(
            [jnp.concatenate([s, zero], axis=1), jnp.concatenate([zero, s], axis=1)], axis=0
        )
        own[x, y, plane * CL + c] = nt(a, b).astype(BF16)

    pl.semaphore_wait(barrier, len(friends))

    slots = [0]

    def send(src, dst, dev):
        i = slots[0]
        slots[0] += 1
        copy = pltpu.make_async_remote_copy(
            src_ref=src, dst_ref=dst, send_sem=send_sem.at[i], recv_sem=recv_sem.at[i],
            device_id=dev, device_id_type=MESH,
        )
        copy.start()
        return copy

    everything = []

    def send_all(items):
        copies = [send(*item) for item in items]
        everything.extend(copies)
        return copies

    def arrived(copies):
        for copy in copies:
            copy.wait_recv()

    block = own.at[x, y, mine]
    z_far, = send_all([(block, block, opposite)])
    z_near, = send_all([(block, neighbour.at[x, y, mine], near_z)])
    a1 = send_all([(block, block, dev) for _, dev in x_peers])
    h_after, = send_all([(sig.at[CL - 1], halo.at[0], after_dev)])
    h_before, = send_all([(sig.at[0], halo.at[1], before_dev)])

    t_count, a_count, j_count = 16, 4, 32
    size = t_count * j_count
    perm1[...] = one_hot(size, size, lambda r: (r % j_count) * t_count + r // j_count)

    def column_of(c):
        kp, h, rest = c // 256, (c // 128) % 2, c % 128
        return (rest // HALF) * 128 + kp * 64 + h * HALF + rest % HALF

    r_i = lax.broadcasted_iota(jnp.int32, (size, size), 0)
    c_i = lax.broadcasted_iota(jnp.int32, (size, size), 1)
    perm2[...] = jnp.where(r_i == column_of(c_i), 1.0, 0.0).astype(BF16)
    reorder = one_hot(R, R, lambda r: (r % HALF) * 2 + r // HALF)
    for c in range(CL):
        leaf_perm[c] = nn(reorder, leaf[c]).astype(BF16)

    places = (1, jnp.where(core == 0, 2, 0), jnp.where(core == 0, 0, 2))

    def prepare(s):
        first = pl.multiple_of(places[s] * GSLOTS, GSLOTS)
        x_rows = []
        for j in range(j_count):
            x_rows.append(jnp.concatenate(
                [coup[pl.ds(first + a * t_count, t_count), j * LANES : (j + 1) * LANES]
                 for a in range(a_count)], axis=1))
        xs = jnp.concatenate(x_rows, axis=0)
        ys = nn(perm1[...], xs).astype(BF16)
        ws = nn(ys, perm2[...]).astype(BF16)
        lane_slot = lax.broadcasted_iota(jnp.int32, (1, LANES), 1) // HALF
        for t in range(t_count):
            code = jnp.full((1, LANES), -1, jnp.int32)
            for a in range(a_count):
                b = first + a * t_count + t
                here = jnp.where(live_ref[b] != 0, rows_ref[b], -1)
                code = jnp.where(lane_slot == a, here, code)
            for i in range(CL):
                mask = jnp.where(code == i, 1.0, 0.0)
                mask = jnp.broadcast_to(mask, (j_count, LANES)).astype(BF16)
                for kp in range(2):
                    for h in range(2):
                        tile = ws[t * j_count : (t + 1) * j_count,
                                  (kp * 2 + h) * LANES : (kp * 2 + h + 1) * LANES]
                        lhs[s, (h * CL + i) * R + kp * HALF : (h * CL + i) * R + (kp + 1) * HALF,
                            t * LANES : (t + 1) * LANES] = tile * mask

    def multiply(s, panel):
        first = places[s] * GSLOTS
        for t in range(t_count):
            for a in range(a_count):
                c = lax.rem(cols_ref[first + a * t_count + t], n_row * CL)
                at = (t * a_count + a) * HALF
                gathered[at : at + HALF] = panel[c // (8 * ny), (c // 8) % ny, c % 8]
        part = nn(lhs[s], gathered[...])
        if s == 0:
            acc[...] = part
        else:
            acc[...] += part

    stage[2].wait()
    prepare(0)

    z_near.wait_recv()
    n_block = neighbour.at[x, y, next_mine]
    n1 = send_all([(n_block, n_block, dev) for _, dev in y_peers])
    arrived(a1)
    a_column = own.at[:, y, mine]
    a2 = send_all([(a_column, a_column, dev) for _, dev in y_peers])

    z_far.wait_recv()
    lower, upper = pl.ds(other_start, 2), pl.ds(other_start + 2, 2)
    b1y = send_all([(own.at[x, y, lower], own.at[x, y, lower], dev) for _, dev in y_peers])
    b1x = send_all([(own.at[x, y, upper], own.at[x, y, upper], dev) for _, dev in x_peers])
    prepare(1)

    arrived(n1)
    n_row_ref = neighbour.at[x, :, next_mine]
    n2 = send_all([(n_row_ref, n_row_ref, dev) for _, dev in x_peers])
    arrived(b1y)
    b_row = own.at[x, :, lower]
    b2x = send_all([(b_row, b_row, dev) for _, dev in x_peers])
    fwd = send_all([(b_row, neighbour.at[x, :, lower], near_z)])
    arrived(b1x)
    b_col = own.at[:, y, upper]
    b2y = send_all([(b_col, b_col, dev) for _, dev in y_peers])
    fwd += send_all([(b_col, neighbour.at[:, y, upper], near_z)])
    prepare(2)

    arrived(a2)
    s_all = send_all([(own.at[:, :, mine], sibling.at[:, :, mine], sib)])
    for (px, _), copy in zip(x_peers, b2x):
        from_x = (x + nx - (px - x)) % nx
        copy.wait_recv()
        fwd += send_all([(own.at[from_x, :, lower], neighbour.at[from_x, :, lower], near_z)])
    for (py, _), copy in zip(y_peers, b2y):
        from_y = (y + ny - (py - y)) % ny
        copy.wait_recv()
        fwd += send_all([(own.at[:, from_y, upper], neighbour.at[:, from_y, upper], near_z)])
    other = pl.ds(other_start, CL)
    s_all += send_all([(own.at[:, :, other], sibling.at[:, :, other], sib)])

    stage[3].wait()
    h_after.wait_recv()
    h_before.wait_recv()
    left = jnp.where(linear == 0, jnp.zeros_like(zero), halo[0])
    right = jnp.where(linear == count - 1, jnp.zeros_like(zero), halo[1])
    signals = [left] + [sig[c] for c in range(CL)] + [right]
    for c in range(CL):
        wide = jnp.concatenate(signals[c : c + 3], axis=1)
        weights = jnp.concatenate([near[c, i] for i in range(3)], axis=1)
        total[c] = nt(wide, weights)

    multiply(0, own)
    arrived(s_all)
    multiply(1, sibling)
    arrived(n2)
    arrived(fwd)
    multiply(2, neighbour)

    both = acc[0 : CL * R] + pltpu.roll(acc[CL * R :], R, 1)
    far = both[:, 0:R].astype(BF16)
    for c in range(CL):
        part = lax.dot_general(
            far[c * R : (c + 1) * R], leaf_perm[c], (((0,), (0,)), ((), ())),
            preferred_element_type=F32,
        )
        out_ref[c] = (total[c] + part).astype(BF16)
    for copy in everything:
        copy.wait_send()


def per_device(nx, ny, nz, signal, leaf_basis, near_blocks, coupling, block_cols, block_rows, block_live):
    smem = pl.BlockSpec(memory_space=pltpu.SMEM)
    hbm = pl.BlockSpec(memory_space=pltpu.HBM)
    panel = pltpu.VMEM((nx, ny, 2 * CL, HALF, LANES), BF16)
    copies = 64
    return pl.pallas_call(
        functools.partial(kernel, nx, ny, nz),
        name="h2_product",
        out_shape=jax.ShapeDtypeStruct((CL, R, LEAF), BF16),
        in_specs=[smem] * 3 + [hbm] * 4,
        out_specs=pl.BlockSpec(memory_space=pltpu.VMEM),
        scratch_shapes=[
            pltpu.VMEM((CL, R, LEAF), BF16),
            pltpu.VMEM((CL, R, LEAF), BF16),
            pltpu.VMEM((CL, 3, LEAF, LEAF), BF16),
            pltpu.VMEM((3 * GSLOTS, R * R), BF16),
            panel, panel, panel,
            pltpu.VMEM((2, R, LEAF), BF16),
            pltpu.VMEM((3, 2 * CL * R, GSLOTS * HALF), BF16),
            pltpu.VMEM((GSLOTS * HALF, LANES), BF16),
            pltpu.VMEM((2 * CL * R, LANES), F32),
            pltpu.VMEM((CL, R, LEAF), F32),
            pltpu.VMEM((512, 512), BF16),
            pltpu.VMEM((512, 512), BF16),
            pltpu.VMEM((CL, R, LEAF), BF16),
            pltpu.SemaphoreType.DMA((4,)),
            pltpu.SemaphoreType.DMA((copies,)),
            pltpu.SemaphoreType.DMA((copies,)),
        ],
        compiler_params=pltpu.CompilerParams(
            collective_id=0, has_side_effects=True, vmem_limit_bytes=48 * 2**20
        ),
    )(block_cols, block_rows, block_live, signal, leaf_basis, near_blocks, coupling)


def solution(mesh, nx=SIDE, ny=SIDE):
    both = ("grp", "row")
    in_specs = (
        P(both, None, None), P(both, None, None), P(both, None, None, None), P(both, None),
        P(both), P(both), P(both),
    )
    nz = mesh.shape["grp"] // 2
    return jax.shard_map(
        functools.partial(per_device, nx, ny, nz), mesh=mesh, in_specs=in_specs,
        out_specs=P(both, None, None), check_vma=False,
    )
```

time: 216 us -> 55.8 us (0.26)
  the two profiles are of different devices: /device:TPU:2 before, /device:TPU:1 now
where the time goes in v1:
time: 55.8 us; the launch traced here: 55.5 us
  Pallas kernels  48.7 us (87%)
  local copies, waits for them, and re-layouts  6.75 us (12%)
    pallas_call x1, Pallas kernels, per_device(): pl.pallas_call(functools.partial(kernel, nx, ny, nz), name='h2_product',...  48.7 us
    unnamed x15, local copies, waits for them, and re-layouts  6.75 us

profile of v1, /device:TPU:1, one launch (start us, length us, event | category | flops | bytes accessed | tf_op | source)
XLA Modules:
  0.0 55.5 jit_solution(15630698470680429249)
XLA Ops:
  0.0 0.0 copy-start
  0.0 1.4 %copy-done = bf16[192,4096]{1,0:T(8,128)(2,1)S(1)} copy-done((bf16[192,4096]{1,0:T(8,128)(2,1)S(1)}, bf16[192,4096]{1,0:T(8,128)(2,1)}, u32[]{:S(2)}) %copy-start) | copy-done | bytes 1572888
  1.4 0.0 copy-start.1
  1.4 1.0 %copy-done.1 = bf16[4,3,128,128]{3,2,1,0:T(8,128)(2,1)S(1)} copy-done((bf16[4,3,128,128]{3,2,1,0:T(8,128)(2,1)S(1)}, bf16[4,3,128,128]{3,2,1,0:T(8,128)(2,1)}, u32[]{:S(2)}) %copy-start.1) | copy-done | bytes 393240
  2.4 0.0 copy-start.2
  2.4 0.8 %copy-done.2 = bf16[4,64,128]{2,1,0:T(8,128)(2,1)S(1)} copy-done((bf16[4,64,128]{2,1,0:T(8,128)(2,1)S(1)}, bf16[4,64,128]{2,1,0:T(8,128)(2,1)}, u32[]{:S(2)}) %copy-start.2) | copy-done | bytes 65560
  3.2 0.0 copy-start.3
  3.2 0.8 %copy-done.3 = bf16[4,64,128]{2,1,0:T(8,128)(2,1)S(1)} copy-done((bf16[4,64,128]{2,1,0:T(8,128)(2,1)S(1)}, bf16[4,64,128]{2,1,0:T(8,128)(2,1)}, u32[]{:S(2)}) %copy-start.3) | copy-done | bytes 65560
  4.1 0.0 copy-start.4
  4.1 0.7 %copy-done.4 = s32[192]{0:T(256)S(1)} copy-done((s32[192]{0:T(256)S(1)}, s32[192]{0:T(256)}, u32[]{:S(2)}) %copy-start.4) | copy-done | bytes 792
  4.8 0.0 copy-start.5
  4.8 0.7 %copy-done.5 = s32[192]{0:T(256)S(1)} copy-done((s32[192]{0:T(256)S(1)}, s32[192]{0:T(256)}, u32[]{:S(2)}) %copy-start.5) | copy-done | bytes 792
  5.4 0.0 copy-start.6
  5.4 0.7 %copy-done.6 = s32[192]{0:T(256)S(1)} copy-done((s32[192]{0:T(256)S(1)}, s32[192]{0:T(256)}, u32[]{:S(2)}) %copy-start.6) | copy-done | bytes 792
  6.1 48.7 %h2_product.1 = bf16[4,64,128]{2,1,0:T(8,128)(2,1)S(1)} custom-call(s32[192]{0:T(256)S(1)} %copy-done.4, s32[192]{0:T(256)S(1)} %copy-done.5, s32[192]{0:T(256)S(1)} %copy-done.6, bf16[4,64,128]{2,1,0:T(8,128)(2,1)S(1)} %copy-done.2, bf16[4,64,128]{2,1,0:T(8,128)(2,1)S(1)} %copy-done.3, bf16[4,3,128,128]{3,2,1,0:T(8,128)(2,1)S(1)} %copy-done.1, ...), custom_call_target="tpu_custom_call" | custom-call | tf_op jit(solution)/shard_map/h2_product/pallas_call | solution.py:260
  54.8 0.6 %copy.9 = bf16[4,64,128]{2,1,0:T(8,128)(2,1)} copy(bf16[4,64,128]{2,1,0:T(8,128)(2,1)S(1)} %h2_product.1) | data formatting | bytes 131072
Async XLA Ops:
  0.0 1.4 %copy-start = (bf16[192,4096]{1,0:T(8,128)(2,1)S(1)}, bf16[192,4096]{1,0:T(8,128)(2,1)}, u32[]{:S(2)}) copy-start(bf16[192,4096]{1,0:T(8,128)(2,1)} %coup_hbm.1) | copy-start | bytes 4718596
  1.4 1.0 %copy-start.1 = (bf16[4,3,128,128]{3,2,1,0:T(8,128)(2,1)S(1)}, bf16[4,3,128,128]{3,2,1,0:T(8,128)(2,1)}, u32[]{:S(2)}) copy-start(bf16[4,3,128,128]{3,2,1,0:T(8,128)(2,1)} %near_hbm.1) | copy-start | bytes 1179652
  2.4 0.8 %copy-start.2 = (bf16[4,64,128]{2,1,0:T(8,128)(2,1)S(1)}, bf16[4,64,128]{2,1,0:T(8,128)(2,1)}, u32[]{:S(2)}) copy-start(bf16[4,64,128]{2,1,0:T(8,128)(2,1)} %sig_hbm.1) | copy-start | bytes 196612
  3.2 0.8 %copy-start.3 = (bf16[4,64,128]{2,1,0:T(8,128)(2,1)S(1)}, bf16[4,64,128]{2,1,0:T(8,128)(2,1)}, u32[]{:S(2)}) copy-start(bf16[4,64,128]{2,1,0:T(8,128)(2,1)} %leaf_hbm.1) | copy-start | bytes 196612
  4.1 0.7 %copy-start.4 = (s32[192]{0:T(256)S(1)}, s32[192]{0:T(256)}, u32[]{:S(2)}) copy-start(s32[192]{0:T(256)} %cols_ref.1) | copy-start | bytes 2308
  4.8 0.7 %copy-start.5 = (s32[192]{0:T(256)S(1)}, s32[192]{0:T(256)}, u32[]{:S(2)}) copy-start(s32[192]{0:T(256)} %rows_ref.1) | copy-start | bytes 2308
  5.4 0.7 %copy-start.6 = (s32[192]{0:T(256)S(1)}, s32[192]{0:T(256)}, u32[]{:S(2)}) copy-start(s32[192]{0:T(256)} %live_ref.1) | copy-start | bytes 2308

commit v2 on v1

v2 whole, which is shorter than its diff:
```python
import functools

import jax
import jax.numpy as jnp
from jax import lax
from jax.experimental import pallas as pl
from jax.experimental.pallas import tpu as pltpu
from jax.sharding import PartitionSpec as P

MESH = pl.DeviceIdType.MESH
F32 = jnp.float32
BF16 = jnp.bfloat16

CL = 4
R = 64
LEAF = 128
GSLOTS = 64
HALF = 32
LANES = 128
SIDE = 4


def one_hot(rows, columns, chosen):
    row = lax.broadcasted_iota(jnp.int32, (rows, columns), 0)
    column = lax.broadcasted_iota(jnp.int32, (rows, columns), 1)
    return jnp.where(column == chosen(row), 1.0, 0.0).astype(BF16)


def ring(n):
    return sorted(range(1, n), key=lambda d: min(d, n - d))


def nt(a, b):
    return lax.dot_general(a, b, (((1,), (1,)), ((), ())), preferred_element_type=F32)


def nn(a, b):
    return jnp.dot(a, b, preferred_element_type=F32)


def kernel(
    nx, ny, nz,
    cols_hbm, rows_hbm, live_hbm, sig_hbm, leaf_hbm, near_hbm, coup_hbm, out_ref,
    cols_ref, rows_ref, live_ref,
    sig, leaf, near, coup, own, sibling, neighbour, halo,
    lhs, gathered, acc, total, perm1, perm2, leaf_perm,
    local_sem, send_sem, recv_sem, hello,
):
    grp = lax.axis_index("grp")
    row = lax.axis_index("row")
    n_grp, n_row = 2 * nz, 2 * nx * ny
    z, core = grp // 2, grp % 2
    xy, plane = row // 2, row % 2
    x, y = xy // ny, xy % ny

    def device(x_, y_, plane_):
        return (grp, (x_ * ny + y_) * 2 + plane_)

    opposite = device(x, y, 1 - plane)
    sib = (z * 2 + 1 - core, row)
    step = 2 * core - 1
    z_here = plane * nz + z
    z_next = (z_here + step + 2 * nz) % (2 * nz)
    next_plane = z_next // nz
    next_grp = (z_next % nz) * 2 + 1 - core
    near_z = (next_grp, xy * 2 + next_plane)
    x_peers = [((x + d) % nx, device((x + d) % nx, y, plane)) for d in ring(nx)]
    y_peers = [((y + d) % ny, device(x, (y + d) % ny, plane)) for d in ring(ny)]
    linear = grp * n_row + row
    count = n_grp * n_row
    after, before = (linear + 1) % count, (linear + count - 1) % count
    edge = jnp.where(plane == 0, before, after)
    edge_dev = (edge // n_row, edge % n_row)

    def key(z_, plane_):
        return jnp.where(plane_ == 0, z_, nz)

    here = key(z, plane)
    k_opp, k_edge = key(z, 1 - plane), key(edge_dev[0] // 2, 1 - plane)
    k_near = key(z_next % nz, next_plane)
    pairs = [
        (dev, here + 1 < there, here > there + 1)
        for dev, there in ((opposite, k_opp), (edge_dev, k_edge), (near_z, k_near))
    ]
    early_opp, early_edge, early_near = [early for _, early, _ in pairs]

    mine = pl.ds(plane * CL, CL)
    other_start = (1 - plane) * CL

    stage = []
    loads = ((leaf_hbm, leaf), (sig_hbm, sig), (coup_hbm, coup), (near_hbm, near),
             (cols_hbm, cols_ref), (rows_hbm, rows_ref), (live_hbm, live_ref))
    for i, (src, dst) in enumerate(loads):
        stage.append(pltpu.make_async_copy(src, dst, local_sem.at[i]))
        stage[-1].start()

    barrier = pltpu.get_barrier_semaphore()

    def greet(semaphore, dev):
        pl.semaphore_signal(semaphore, inc=1, device_id=dev, device_id_type=MESH)

    friends = [sib] + [dev for _, dev in x_peers] + [dev for _, dev in y_peers]
    expected = len(friends)
    for friend in friends:
        greet(barrier, friend)
    for dev, early, late in pairs:
        pl.when(jnp.logical_not(late))(functools.partial(greet, barrier, dev))
        expected = expected + jnp.where(early, 0, 1)

    pl.semaphore_wait(barrier, expected)
    for i, (dev, _, late) in enumerate(pairs):
        pl.when(late)(functools.partial(greet, hello.at[i], dev))

    stage[0].wait()
    stage[1].wait()
    zero = jnp.zeros((R, LEAF), BF16)
    for c in range(CL):
        a = jnp.concatenate([leaf[c, 0:HALF], leaf[c, HALF : 2 * HALF]], axis=1)
        s = sig[c]
        b = jnp.concatenate(
            [jnp.concatenate([s, zero], axis=1), jnp.concatenate([zero, s], axis=1)], axis=0
        )
        own[x, y, plane * CL + c] = nt(a, b).astype(BF16)

    slots = [0]
    everything = []

    def prepared(src, dst, dev):
        i = slots[0]
        slots[0] += 1
        copy = pltpu.make_async_remote_copy(
            src_ref=src, dst_ref=dst, send_sem=send_sem.at[i], recv_sem=recv_sem.at[i],
            device_id=dev, device_id_type=MESH,
        )
        everything.append(copy)
        return copy

    def send_all(items):
        copies = [prepared(*item) for item in items]
        for copy in copies:
            copy.start()
        return copies

    def arrived(copies):
        for copy in copies:
            copy.wait_recv()

    block = own.at[x, y, mine]
    n_dst = neighbour.at[x, y, mine]
    to_opp = prepared(block, block, opposite)
    to_near = prepared(block, n_dst, near_z)
    opp_slot = plane
    halo_opp = prepared(sig.at[(1 - plane) * (CL - 1)], halo.at[opp_slot], opposite)
    halo_edge = prepared(sig.at[plane * (CL - 1)], halo.at[1 - opp_slot], edge_dev)

    def now(early, *copies):
        @pl.when(jnp.logical_not(early))
        def _():
            for copy in copies:
                copy.start()

    def then(i, *copies):
        @pl.when(pairs[i][1])
        def _():
            pl.semaphore_wait(hello.at[i], 1)
            for copy in copies:
                copy.start()

    def spread_first(panel, start):
        low, high = pl.ds(start, 2), pl.ds(start + 2, 2)
        return (
            send_all([(panel.at[x, y, low], panel.at[x, y, low], dev) for _, dev in y_peers]),
            send_all([(panel.at[x, y, high], panel.at[x, y, high], dev) for _, dev in x_peers]),
        )

    def spread_second(panel, start, first):
        low, high = pl.ds(start, 2), pl.ds(start + 2, 2)
        arrived(first[0])
        line = panel.at[x, :, low]
        copies = send_all([(line, line, dev) for _, dev in x_peers])
        arrived(first[1])
        line = panel.at[:, y, high]
        return copies + send_all([(line, line, dev) for _, dev in y_peers])

    now(early_opp, to_opp)
    now(early_near, to_near)
    my_start, next_start = plane * CL, next_plane * CL
    a1 = spread_first(own, my_start)

    t_count, a_count, j_count = 16, 4, 32
    size = t_count * j_count
    perm1[...] = one_hot(size, size, lambda r: (r % j_count) * t_count + r // j_count)

    def column_of(c):
        kp, h, rest = c // 256, (c // 128) % 2, c % 128
        return (rest // HALF) * 128 + kp * 64 + h * HALF + rest % HALF

    r_i = lax.broadcasted_iota(jnp.int32, (size, size), 0)
    c_i = lax.broadcasted_iota(jnp.int32, (size, size), 1)
    perm2[...] = jnp.where(r_i == column_of(c_i), 1.0, 0.0).astype(BF16)
    reorder = one_hot(R, R, lambda r: (r % HALF) * 2 + r // HALF)
    for c in range(CL):
        leaf_perm[c] = nn(reorder, leaf[c]).astype(BF16)

    places = (1, jnp.where(core == 0, 2, 0), jnp.where(core == 0, 0, 2))

    def prepare(s):
        first = pl.multiple_of(places[s] * GSLOTS, GSLOTS)
        x_rows = []
        for j in range(j_count):
            x_rows.append(jnp.concatenate(
                [coup[pl.ds(first + a * t_count, t_count), j * LANES : (j + 1) * LANES]
                 for a in range(a_count)], axis=1))
        xs = jnp.concatenate(x_rows, axis=0)
        ys = nn(perm1[...], xs).astype(BF16)
        ws = nn(ys, perm2[...]).astype(BF16)
        lane_slot = lax.broadcasted_iota(jnp.int32, (1, LANES), 1) // HALF
        for t in range(t_count):
            code = jnp.full((1, LANES), -1, jnp.int32)
            for a in range(a_count):
                b = first + a * t_count + t
                slot_row = jnp.where(live_ref[b] != 0, rows_ref[b], -1)
                code = jnp.where(lane_slot == a, slot_row, code)
            for i in range(CL):
                mask = jnp.where(code == i, 1.0, 0.0)
                mask = jnp.broadcast_to(mask, (j_count, LANES)).astype(BF16)
                for kp in range(2):
                    for h in range(2):
                        tile = ws[t * j_count : (t + 1) * j_count,
                                  (kp * 2 + h) * LANES : (kp * 2 + h + 1) * LANES]
                        lhs[s, (h * CL + i) * R + kp * HALF : (h * CL + i) * R + (kp + 1) * HALF,
                            t * LANES : (t + 1) * LANES] = tile * mask

    def multiply(s, panel):
        first = places[s] * GSLOTS
        for t in range(t_count):
            for a in range(a_count):
                c = lax.rem(cols_ref[first + a * t_count + t], n_row * CL)
                at = (t * a_count + a) * HALF
                gathered[at : at + HALF] = panel[c // (8 * ny), (c // 8) % ny, c % 8]
        part = nn(lhs[s], gathered[...])
        if s == 0:
            acc[...] = part
        else:
            acc[...] += part

    for copy in stage[2:]:
        copy.wait()
    prepare(0)
    a2 = spread_second(own, my_start, a1)
    then(2, to_near)
    to_near.wait_recv()
    n1 = spread_first(neighbour, next_start)
    prepare(1)
    n2 = spread_second(neighbour, next_start, n1)
    then(0, to_opp)
    prepare(2)

    def near_field(c, first, signals):
        wide = jnp.concatenate(signals, axis=1)
        weights = jnp.concatenate([near[c, first + i] for i in range(len(signals))], axis=1)
        return nt(wide, weights)

    for c in range(CL):
        low, high = max(c - 1, 0), min(c + 1, CL - 1)
        total[c] = near_field(c, low - c + 1, [sig[i] for i in range(low, high + 1)])

    now(early_opp, halo_opp)
    now(early_edge, halo_edge)
    to_opp.wait_recv()
    b1 = spread_first(own, other_start)
    pl.when(early_opp)(halo_opp.start)
    then(1, halo_edge)

    low, high = pl.ds(other_start, 2), pl.ds(other_start + 2, 2)

    def forward(at):
        return send_all([(own.at[at], neighbour.at[at], near_z)])

    b2 = spread_second(own, other_start, b1)
    fwd = forward((x, slice(None), low)) + forward((slice(None), y, high))
    arrived(a2)
    s_all = send_all([(own.at[:, :, mine], sibling.at[:, :, mine], sib)])
    for i in range(max(nx, ny) - 1):
        if i < nx - 1:
            b2[i].wait_recv()
            fwd += forward(((x + nx - ring(nx)[i]) % nx, slice(None), low))
        if i < ny - 1:
            b2[nx - 1 + i].wait_recv()
            fwd += forward((slice(None), (y + ny - ring(ny)[i]) % ny, high))
    other = pl.ds(other_start, CL)
    s_all += send_all([(own.at[:, :, other], sibling.at[:, :, other], sib)])
    multiply(0, own)
    arrived(s_all)
    multiply(1, sibling)
    arrived(n2)
    arrived(fwd)
    multiply(2, neighbour)

    halo_opp.wait_recv()
    halo_edge.wait_recv()
    left = jnp.where(linear == 0, jnp.zeros_like(zero), halo[0])
    right = jnp.where(linear == count - 1, jnp.zeros_like(zero), halo[1])
    total[0] += near_field(0, 0, [left])
    total[CL - 1] += near_field(CL - 1, 2, [right])

    both = acc[0 : CL * R] + pltpu.roll(acc[CL * R :], R, 1)
    far = both[:, 0:R].astype(BF16)
    for c in range(CL):
        part = lax.dot_general(
            far[c * R : (c + 1) * R], leaf_perm[c], (((0,), (0,)), ((), ())),
            preferred_element_type=F32,
        )
        out_ref[c] = (total[c] + part).astype(BF16)
    for copy in everything:
        copy.wait_send()


def per_device(nx, ny, nz, signal, leaf_basis, near_blocks, coupling, block_cols, block_rows, block_live):
    index = pltpu.SMEM((3 * GSLOTS,), jnp.int32)
    hbm = pl.BlockSpec(memory_space=pltpu.HBM)
    panel = pltpu.VMEM((nx, ny, 2 * CL, HALF, LANES), BF16)
    copies = 64
    return pl.pallas_call(
        functools.partial(kernel, nx, ny, nz),
        name="h2_product",
        out_shape=jax.ShapeDtypeStruct((CL, R, LEAF), BF16),
        in_specs=[hbm] * 7,
        out_specs=pl.BlockSpec(memory_space=pltpu.VMEM),
        scratch_shapes=[
            index, index, index,
            pltpu.VMEM((CL, R, LEAF), BF16),
            pltpu.VMEM((CL, R, LEAF), BF16),
            pltpu.VMEM((CL, 3, LEAF, LEAF), BF16),
            pltpu.VMEM((3 * GSLOTS, R * R), BF16),
            panel, panel, panel,
            pltpu.VMEM((2, R, LEAF), BF16),
            pltpu.VMEM((3, 2 * CL * R, GSLOTS * HALF), BF16),
            pltpu.VMEM((GSLOTS * HALF, LANES), BF16),
            pltpu.VMEM((2 * CL * R, LANES), F32),
            pltpu.VMEM((CL, R, LEAF), F32),
            pltpu.VMEM((512, 512), BF16),
            pltpu.VMEM((512, 512), BF16),
            pltpu.VMEM((CL, R, LEAF), BF16),
            pltpu.SemaphoreType.DMA((7,)),
            pltpu.SemaphoreType.DMA((copies,)),
            pltpu.SemaphoreType.DMA((copies,)),
            pltpu.SemaphoreType.REGULAR((3,)),
        ],
        compiler_params=pltpu.CompilerParams(
            collective_id=0, has_side_effects=True, vmem_limit_bytes=60 * 2**20
        ),
    )(block_cols, block_rows, block_live, signal, leaf_basis, near_blocks, coupling)


def solution(mesh, nx=SIDE, ny=SIDE):
    both = ("grp", "row")
    in_specs = (
        P(both, None, None), P(both, None, None), P(both, None, None, None), P(both, None),
        P(both), P(both), P(both),
    )
    nz = mesh.shape["grp"] // 2
    return jax.shard_map(
        functools.partial(per_device, nx, ny, nz), mesh=mesh, in_specs=in_specs,
        out_specs=P(both, None, None), check_vma=False,
    )
```

time: 55.8 us -> 44.7 us (0.80)
  the two profiles are of different devices: /device:TPU:1 before, /device:TPU:241 now
where the time goes in v2:
time: 44.7 us; the launch traced here: 44.6 us
  Pallas kernels  43.1 us (96%)
  local copies, waits for them, and re-layouts  1.47 us (3%)
    pallas_call x1, Pallas kernels, per_device(): pl.pallas_call(functools.partial(kernel, nx, ny, nz), name='h2_product',...  43.1 us
    unnamed x1, local copies, waits for them, and re-layouts  1.47 us

profile of v2, /device:TPU:241, one launch (start us, length us, event | category | flops | bytes accessed | tf_op | source)
XLA Modules:
  0.0 44.6 jit_solution(15228589428758746017)
XLA Ops:
  0.0 43.1 %h2_product.1 = bf16[4,64,128]{2,1,0:T(8,128)(2,1)} custom-call(s32[192]{0:T(256)} %cols_hbm.1, s32[192]{0:T(256)} %rows_hbm.1, s32[192]{0:T(256)} %live_hbm.1, bf16[4,64,128]{2,1,0:T(8,128)(2,1)} %sig_hbm.1, bf16[4,64,128]{2,1,0:T(8,128)(2,1)} %leaf_hbm.1, bf16[4,3,128,128]{3,2,1,0:T(8,128)(2,1)} %near_hbm.1, bf16[192,4096]{1,0:T(8,128)(2,1)} %coup_hbm.1), custom_call_target="tpu_custom_call" | custom-call | tf_op jit(solution)/shard_map/h2_product/pallas_call | solution.py:324
  43.1 1.5 %copy.9 = bf16[4,64,128]{2,1,0:T(8,128)(2,1)} copy(bf16[4,64,128]{2,1,0:T(8,128)(2,1)} %h2_product.1) | data formatting | bytes 131072

commit v3 on v2

--- a/solution.py
+++ b/solution.py
@@ -79,10 +79,15 @@
     k_opp, k_edge = key(z, 1 - plane), key(edge_dev[0] // 2, 1 - plane)
     k_near = key(z_next % nz, next_plane)
     pairs = [
-        (dev, here + 1 < there, here > there + 1)
-        for dev, there in ((opposite, k_opp), (edge_dev, k_edge), (near_z, k_near))
+        (opposite, here < k_opp, here > k_opp),
+        (edge_dev, here < k_edge, here > k_edge),
+        (near_z, here + 1 < k_near, here > k_near + 1),
     ]
     early_opp, early_edge, early_near = [early for _, early, _ in pairs]
+    late_near = pairs[2][2]
+    special = early_near
+    giver = jnp.logical_and(plane == 0, linear // n_row == n_grp - 1)
+    taker = (jnp.where(giver, 0, grp), jnp.where(giver, row, opposite[1]))
 
     mine = pl.ds(plane * CL, CL)
     other_start = (1 - plane) * CL
@@ -106,6 +111,8 @@
     for dev, early, late in pairs:
         pl.when(jnp.logical_not(late))(functools.partial(greet, barrier, dev))
         expected = expected + jnp.where(early, 0, 1)
+    pl.when(special)(functools.partial(greet, barrier, (n_grp - 1, row)))
+    expected = expected + jnp.where(giver, 1, 0)
 
     pl.semaphore_wait(barrier, expected)
     for i, (dev, _, late) in enumerate(pairs):
@@ -125,14 +132,14 @@
     slots = [0]
     everything = []
 
-    def prepared(src, dst, dev):
+    def prepared(src, dst, dev, when=None):
         i = slots[0]
         slots[0] += 1
         copy = pltpu.make_async_remote_copy(
             src_ref=src, dst_ref=dst, send_sem=send_sem.at[i], recv_sem=recv_sem.at[i],
             device_id=dev, device_id_type=MESH,
         )
-        everything.append(copy)
+        everything.append((copy, when))
         return copy
 
     def send_all(items):
@@ -166,26 +173,40 @@
             for copy in copies:
                 copy.start()
 
-    def spread_first(panel, start):
+    def first_copies(panel, start, when=None):
         low, high = pl.ds(start, 2), pl.ds(start + 2, 2)
         return (
-            send_all([(panel.at[x, y, low], panel.at[x, y, low], dev) for _, dev in y_peers]),
-            send_all([(panel.at[x, y, high], panel.at[x, y, high], dev) for _, dev in x_peers]),
+            [prepared(panel.at[x, y, low], panel.at[x, y, low], dev, when) for _, dev in y_peers],
+            [prepared(panel.at[x, y, high], panel.at[x, y, high], dev, when) for _, dev in x_peers],
         )
 
-    def spread_second(panel, start, first):
-        low, high = pl.ds(start, 2), pl.ds(start + 2, 2)
-        arrived(first[0])
-        line = panel.at[x, :, low]
-        copies = send_all([(line, line, dev) for _, dev in x_peers])
-        arrived(first[1])
-        line = panel.at[:, y, high]
-        return copies + send_all([(line, line, dev) for _, dev in y_peers])
-
+    def second_copies(panel, start, when=None):
+        low, high = panel.at[x, :, pl.ds(start, 2)], panel.at[:, y, pl.ds(start + 2, 2)]
+        return (
+            [prepared(low, low, dev, when) for _, dev in x_peers],
+            [prepared(high, high, dev, when) for _, dev in y_peers],
+        )
+
+    def begin(copies):
+        for copy in copies:
+            copy.start()
+
+    def pass_on(first, second):
+        for got, give in zip(first, second):
+            arrived(got)
+            begin(give)
+
+    to_taker = prepared(block, n_dst, taker, giver)
     now(early_opp, to_opp)
+    pl.when(giver)(to_taker.start)
     now(early_near, to_near)
     my_start, next_start = plane * CL, next_plane * CL
-    a1 = spread_first(own, my_start)
+    a1, a2 = first_copies(own, my_start), second_copies(own, my_start)
+    n1, n2 = first_copies(neighbour, next_start), second_copies(neighbour, next_start)
+    b1 = first_copies(own, other_start)
+    next_other = (1 - next_plane) * CL
+    t1, t2 = first_copies(neighbour, next_other, special), second_copies(neighbour, next_other, special)
+    begin(a1[0] + a1[1])
 
     t_count, a_count, j_count = 16, 4, 32
     size = t_count * j_count
@@ -247,14 +268,29 @@
     for copy in stage[2:]:
         copy.wait()
     prepare(0)
-    a2 = spread_second(own, my_start, a1)
+    pass_on(a1, a2)
+
     then(2, to_near)
     to_near.wait_recv()
-    n1 = spread_first(neighbour, next_start)
+    begin(n1[0] + n1[1])
     prepare(1)
-    n2 = spread_second(neighbour, next_start, n1)
     then(0, to_opp)
+
+    def far_step():
+        to_opp.wait_recv()
+        begin(b1[0] + b1[1])
+
+    @pl.when(special)
+    def _():
+        to_taker.wait_recv()
+        begin(t1[0] + t1[1])
+        far_step()
+
+    pass_on(n1, n2)
     prepare(2)
+    halo_opp.start()
+    then(1, halo_edge)
+    now(early_edge, halo_edge)
 
     def near_field(c, first, signals):
         wide = jnp.concatenate(signals, axis=1)
@@ -265,36 +301,63 @@
         low, high = max(c - 1, 0), min(c + 1, CL - 1)
         total[c] = near_field(c, low - c + 1, [sig[i] for i in range(low, high + 1)])
 
-    now(early_opp, halo_opp)
-    now(early_edge, halo_edge)
-    to_opp.wait_recv()
-    b1 = spread_first(own, other_start)
-    pl.when(early_opp)(halo_opp.start)
-    then(1, halo_edge)
-
-    low, high = pl.ds(other_start, 2), pl.ds(other_start + 2, 2)
+    pl.when(jnp.logical_not(special))(far_step)
+
+    start = other_start
+    usual = jnp.logical_not(special)
+    forwards = jnp.logical_not(late_near)
+    pair_low, pair_high = pl.ds(start, 2), pl.ds(start + 2, 2)
+    every = slice(None)
 
     def forward(at):
-        return send_all([(own.at[at], neighbour.at[at], near_z)])
-
-    b2 = spread_second(own, other_start, b1)
-    fwd = forward((x, slice(None), low)) + forward((slice(None), y, high))
-    arrived(a2)
-    s_all = send_all([(own.at[:, :, mine], sibling.at[:, :, mine], sib)])
+        copy = prepared(own.at[at], neighbour.at[at], near_z, forwards)
+        pl.when(forwards)(copy.start)
+        return [copy]
+
+    def share(at):
+        return send_all([(own.at[at], sibling.at[at], sib)])
+
+    arrived(b1[0])
+    line = own.at[x, :, pair_low]
+    b2x = send_all([(line, line, dev) for _, dev in x_peers])
+    f_low, = forward((x, every, pair_low))
+    arrived(b1[1])
+    line = own.at[:, y, pair_high]
+    b2y = send_all([(line, line, dev) for _, dev in y_peers])
+    f_high, = forward((every, y, pair_high))
+    s_all = share((x, every, pair_low)) + share((every, y, pair_high))
+    arrived(a2[0] + a2[1])
+    s_all += share((every, every, mine))
+    m_low = neighbour.at[x, :, pl.ds(next_other, 1)]
+    m_high = neighbour.at[:, y, pl.ds(next_other + 2, 1)]
+    m2 = (
+        [prepared(m_low, m_low, dev, usual) for _, dev in x_peers],
+        [prepared(m_high, m_high, dev, usual) for _, dev in y_peers],
+    )
+
+    def spread_next():
+        pass_on(([f_low], [f_high]), m2)
+
+    pl.when(usual)(spread_next)
+    pl.when(special)(functools.partial(pass_on, t1, t2))
+    fwd = []
     for i in range(max(nx, ny) - 1):
         if i < nx - 1:
-            b2[i].wait_recv()
-            fwd += forward(((x + nx - ring(nx)[i]) % nx, slice(None), low))
+            b2x[i].wait_recv()
+            px = (x + nx - ring(nx)[i]) % nx
+            fwd += forward((px, every, pl.ds(start + 1, 1)))
+            s_all += share((px, every, pair_low))
         if i < ny - 1:
-            b2[nx - 1 + i].wait_recv()
-            fwd += forward((slice(None), (y + ny - ring(ny)[i]) % ny, high))
-    other = pl.ds(other_start, CL)
-    s_all += send_all([(own.at[:, :, other], sibling.at[:, :, other], sib)])
+            b2y[i].wait_recv()
+            py = (y + ny - ring(ny)[i]) % ny
+            fwd += forward((every, py, pl.ds(start + 3, 1)))
+            s_all += share((every, py, pair_high))
     multiply(0, own)
     arrived(s_all)
     multiply(1, sibling)
-    arrived(n2)
-    arrived(fwd)
+    arrived(n2[0] + n2[1])
+    pl.when(usual)(functools.partial(arrived, m2[0] + m2[1] + fwd))
+    pl.when(special)(functools.partial(arrived, t2[0] + t2[1]))
     multiply(2, neighbour)
 
     halo_opp.wait_recv()
@@ -312,15 +375,18 @@
             preferred_element_type=F32,
         )
         out_ref[c] = (total[c] + part).astype(BF16)
-    for copy in everything:
-        copy.wait_send()
+    for copy, when in everything:
+        if when is None:
+            copy.wait_send()
+        else:
+            pl.when(when)(copy.wait_send)
 
 
 def per_device(nx, ny, nz, signal, leaf_basis, near_blocks, coupling, block_cols, block_rows, block_live):
     index = pltpu.SMEM((3 * GSLOTS,), jnp.int32)
     hbm = pl.BlockSpec(memory_space=pltpu.HBM)
     panel = pltpu.VMEM((nx, ny, 2 * CL, HALF, LANES), BF16)
-    copies = 64
+    copies = 96
     return pl.pallas_call(
         functools.partial(kernel, nx, ny, nz),
         name="h2_product",

time: 44.7 us -> 42.6 us (0.953)
  the two profiles are of different devices: /device:TPU:241 before, /device:TPU:1 now
where the time goes in v3:
time: 42.6 us; the launch traced here: 42.5 us
  Pallas kernels  41 us (96%)
  local copies, waits for them, and re-layouts  1.47 us (3%)
    pallas_call x1, Pallas kernels, per_device(): pl.pallas_call(functools.partial(kernel, nx, ny, nz), name='h2_product',...  41 us
    unnamed x1, local copies, waits for them, and re-layouts  1.47 us

profile of v3, /device:TPU:1, one launch (start us, length us, event | category | flops | bytes accessed | tf_op | source)
XLA Modules:
  0.0 42.5 jit_solution(7505470387670181578)
XLA Ops:
  0.0 41.0 %h2_product.1 = bf16[4,64,128]{2,1,0:T(8,128)(2,1)} custom-call(s32[192]{0:T(256)} %cols_hbm.1, s32[192]{0:T(256)} %rows_hbm.1, s32[192]{0:T(256)} %live_hbm.1, bf16[4,64,128]{2,1,0:T(8,128)(2,1)} %sig_hbm.1, bf16[4,64,128]{2,1,0:T(8,128)(2,1)} %leaf_hbm.1, bf16[4,3,128,128]{3,2,1,0:T(8,128)(2,1)} %near_hbm.1, bf16[192,4096]{1,0:T(8,128)(2,1)} %coup_hbm.1), custom_call_target="tpu_custom_call" | custom-call | tf_op jit(solution)/shard_map/h2_product/pallas_call | solution.py:390
  41.0 1.5 %copy.9 = bf16[4,64,128]{2,1,0:T(8,128)(2,1)} copy(bf16[4,64,128]{2,1,0:T(8,128)(2,1)} %h2_product.1) | data formatting | bytes 131072

commit v4 on v3

--- a/solution.py
+++ b/solution.py
@@ -254,11 +254,14 @@
 
     def multiply(s, panel):
         first = places[s] * GSLOTS
+        x_shift = 3 + ny.bit_length() - 1
         for t in range(t_count):
             for a in range(a_count):
-                c = lax.rem(cols_ref[first + a * t_count + t], n_row * CL)
+                c = cols_ref[first + a * t_count + t]
                 at = (t * a_count + a) * HALF
-                gathered[at : at + HALF] = panel[c // (8 * ny), (c // 8) % ny, c % 8]
+                gathered[at : at + HALF] = panel[
+                    (c >> x_shift) & (nx - 1), (c >> 3) & (ny - 1), c & (2 * CL - 1)
+                ]
         part = nn(lhs[s], gathered[...])
         if s == 0:
             acc[...] = part
@@ -270,11 +273,16 @@
     prepare(0)
     pass_on(a1, a2)
 
+
+    def pair_up():
+        then(0, to_opp)
+
+    pl.when(special)(pair_up)
     then(2, to_near)
     to_near.wait_recv()
     begin(n1[0] + n1[1])
     prepare(1)
-    then(0, to_opp)
+    pl.when(jnp.logical_not(special))(pair_up)
 
     def far_step():
         to_opp.wait_recv()
@@ -288,8 +296,7 @@
 
     pass_on(n1, n2)
     prepare(2)
-    halo_opp.start()
-    then(1, halo_edge)
+    now(early_opp, halo_opp)
     now(early_edge, halo_edge)
 
     def near_field(c, first, signals):
@@ -325,6 +332,8 @@
     line = own.at[:, y, pair_high]
     b2y = send_all([(line, line, dev) for _, dev in y_peers])
     f_high, = forward((every, y, pair_high))
+    pl.when(early_opp)(halo_opp.start)
+    then(1, halo_edge)
     s_all = share((x, every, pair_low)) + share((every, y, pair_high))
     arrived(a2[0] + a2[1])
     s_all += share((every, every, mine))
@@ -352,13 +361,18 @@
             py = (y + ny - ring(ny)[i]) % ny
             fwd += forward((every, py, pl.ds(start + 3, 1)))
             s_all += share((every, py, pair_high))
+    def multiply_next():
+        arrived(n2[0] + n2[1])
+        pl.when(usual)(functools.partial(arrived, m2[0] + m2[1] + fwd))
+        pl.when(special)(functools.partial(arrived, t2[0] + t2[1]))
+        multiply(2, neighbour)
+
     multiply(0, own)
+    first_plane = jnp.logical_and(plane == 0, z == 0)
+    pl.when(first_plane)(multiply_next)
     arrived(s_all)
     multiply(1, sibling)
-    arrived(n2[0] + n2[1])
-    pl.when(usual)(functools.partial(arrived, m2[0] + m2[1] + fwd))
-    pl.when(special)(functools.partial(arrived, t2[0] + t2[1]))
-    multiply(2, neighbour)
+    pl.when(jnp.logical_not(first_plane))(multiply_next)
 
     halo_opp.wait_recv()
     halo_edge.wait_recv()

time: 42.6 us -> 40.9 us (0.960)
  Pallas kernels: 41 us -> 39.2 us
    pallas_call x1, Pallas kernels: 41 us -> 39.2 us  [per_device(): pl.pallas_call(functools.partial(kernel, nx, ny, nz), name='h2_product',...]
where the time goes in v4:
time: 40.9 us; the launch traced here: 40.7 us
  Pallas kernels  39.2 us (96%)
  local copies, waits for them, and re-layouts  1.47 us (4%)
    pallas_call x1, Pallas kernels, per_device(): pl.pallas_call(functools.partial(kernel, nx, ny, nz), name='h2_product',...  39.2 us
    unnamed x1, local copies, waits for them, and re-layouts  1.47 us

profile of v4, /device:TPU:1, one launch (start us, length us, event | category | flops | bytes accessed | tf_op | source)
XLA Modules:
  0.0 40.7 jit_solution(11434912213764545821)
XLA Ops:
  0.0 39.2 %h2_product.1 = bf16[4,64,128]{2,1,0:T(8,128)(2,1)} custom-call(s32[192]{0:T(256)} %cols_hbm.1, s32[192]{0:T(256)} %rows_hbm.1, s32[192]{0:T(256)} %live_hbm.1, bf16[4,64,128]{2,1,0:T(8,128)(2,1)} %sig_hbm.1, bf16[4,64,128]{2,1,0:T(8,128)(2,1)} %leaf_hbm.1, bf16[4,3,128,128]{3,2,1,0:T(8,128)(2,1)} %near_hbm.1, bf16[192,4096]{1,0:T(8,128)(2,1)} %coup_hbm.1), custom_call_target="tpu_custom_call" | custom-call | tf_op jit(solution)/shard_map/h2_product/pallas_call | solution.py:404
  39.2 1.5 %copy.9 = bf16[4,64,128]{2,1,0:T(8,128)(2,1)} copy(bf16[4,64,128]{2,1,0:T(8,128)(2,1)} %h2_product.1) | data formatting | bytes 131072

commit v5 on v4

--- a/solution.py
+++ b/solution.py
@@ -295,10 +295,12 @@
         far_step()
 
     pass_on(n1, n2)
-    prepare(2)
     now(early_opp, halo_opp)
     now(early_edge, halo_edge)
 
+    pl.when(jnp.logical_not(special))(far_step)
+
+    prepare(2)
     def near_field(c, first, signals):
         wide = jnp.concatenate(signals, axis=1)
         weights = jnp.concatenate([near[c, first + i] for i in range(len(signals))], axis=1)
@@ -307,8 +309,6 @@
     for c in range(CL):
         low, high = max(c - 1, 0), min(c + 1, CL - 1)
         total[c] = near_field(c, low - c + 1, [sig[i] for i in range(low, high + 1)])
-
-    pl.when(jnp.logical_not(special))(far_step)
 
     start = other_start
     usual = jnp.logical_not(special)
@@ -324,6 +324,8 @@
     def share(at):
         return send_all([(own.at[at], sibling.at[at], sib)])
 
+    arrived(a2[0] + a2[1])
+    s_all = share((every, every, mine))
     arrived(b1[0])
     line = own.at[x, :, pair_low]
     b2x = send_all([(line, line, dev) for _, dev in x_peers])
@@ -334,9 +336,7 @@
     f_high, = forward((every, y, pair_high))
     pl.when(early_opp)(halo_opp.start)
     then(1, halo_edge)
-    s_all = share((x, every, pair_low)) + share((every, y, pair_high))
-    arrived(a2[0] + a2[1])
-    s_all += share((every, every, mine))
+    s_all += share((x, every, pair_low)) + share((every, y, pair_high))
     m_low = neighbour.at[x, :, pl.ds(next_other, 1)]
     m_high = neighbour.at[:, y, pl.ds(next_other + 2, 1)]
     m2 = (
@@ -354,13 +354,13 @@
         if i < nx - 1:
             b2x[i].wait_recv()
             px = (x + nx - ring(nx)[i]) % nx
+            s_all += share((px, every, pair_low))
             fwd += forward((px, every, pl.ds(start + 1, 1)))
-            s_all += share((px, every, pair_low))
         if i < ny - 1:
             b2y[i].wait_recv()
             py = (y + ny - ring(ny)[i]) % ny
+            s_all += share((every, py, pair_high))
             fwd += forward((every, py, pl.ds(start + 3, 1)))
-            s_all += share((every, py, pair_high))
     def multiply_next():
         arrived(n2[0] + n2[1])
         pl.when(usual)(functools.partial(arrived, m2[0] + m2[1] + fwd))
@@ -368,18 +368,18 @@
         multiply(2, neighbour)
 
     multiply(0, own)
-    first_plane = jnp.logical_and(plane == 0, z == 0)
-    pl.when(first_plane)(multiply_next)
-    arrived(s_all)
-    multiply(1, sibling)
-    pl.when(jnp.logical_not(first_plane))(multiply_next)
-
     halo_opp.wait_recv()
     halo_edge.wait_recv()
     left = jnp.where(linear == 0, jnp.zeros_like(zero), halo[0])
     right = jnp.where(linear == count - 1, jnp.zeros_like(zero), halo[1])
     total[0] += near_field(0, 0, [left])
     total[CL - 1] += near_field(CL - 1, 2, [right])
+
+    first_plane = jnp.logical_and(plane == 0, z == 0)
+    pl.when(first_plane)(multiply_next)
+    arrived(s_all)
+    multiply(1, sibling)
+    pl.when(jnp.logical_not(first_plane))(multiply_next)
 
     both = acc[0 : CL * R] + pltpu.roll(acc[CL * R :], R, 1)
     far = both[:, 0:R].astype(BF16)

time: 40.9 us -> 40.9 us (level)
  no operation moved by 1% of the time
where the time goes in v5:
time: 40.9 us; the launch traced here: 40.7 us
  Pallas kernels  39.2 us (96%)
  local copies, waits for them, and re-layouts  1.47 us (4%)
    pallas_call x1, Pallas kernels, per_device(): pl.pallas_call(functools.partial(kernel, nx, ny, nz), name='h2_product',...  39.2 us
    unnamed x1, local copies, waits for them, and re-layouts  1.47 us

profile of v5, /device:TPU:1, one launch (start us, length us, event | category | flops | bytes accessed | tf_op | source)
XLA Modules:
  0.0 40.7 jit_solution(10816691486445705939)
XLA Ops:
  0.0 39.2 %h2_product.1 = bf16[4,64,128]{2,1,0:T(8,128)(2,1)} custom-call(s32[192]{0:T(256)} %cols_hbm.1, s32[192]{0:T(256)} %rows_hbm.1, s32[192]{0:T(256)} %live_hbm.1, bf16[4,64,128]{2,1,0:T(8,128)(2,1)} %sig_hbm.1, bf16[4,64,128]{2,1,0:T(8,128)(2,1)} %leaf_hbm.1, bf16[4,3,128,128]{3,2,1,0:T(8,128)(2,1)} %near_hbm.1, bf16[192,4096]{1,0:T(8,128)(2,1)} %coup_hbm.1), custom_call_target="tpu_custom_call" | custom-call | tf_op jit(solution)/shard_map/h2_product/pallas_call | solution.py:404
  39.2 1.5 %copy.9 = bf16[4,64,128]{2,1,0:T(8,128)(2,1)} copy(bf16[4,64,128]{2,1,0:T(8,128)(2,1)} %h2_product.1) | data formatting | bytes 131072
